TPU v7x, 32 devices: a whole 2x2x4 slice. The times are simulated.
32 devices in a mesh: outer: 4 (over y, core), inner: 8 (over z, x).
Axes of the slice: x: 2, y: 2, z: 4, core: 2. Of those that a mesh axis runs over, the one named last changes fastest.
Arguments:
- matrix_panel: float32 [32, 65536], P(None, ('outer', 'inner')), may hold values from -6 to 6
- row_signs: int32 [65536], P(('outer', 'inner')), may hold values from -1 to 1, as said below
- kept_rows: int32 [4096], replicated, may hold values from 0 to 65535, as said below
Outputs:
- sketch: float32 [4096, 32], P(('outer', 'inner'))
Inputs may be any that keep to these rules, and one draw needn't show every extreme that they name: `row_signs`: each entry is -1 or 1. `kept_rows`: distinct row numbers.
All inputs are finite; a program needn't handle non-finite values.
Results may differ from a plain program's by a relative error of at most 0.00007.
Values sent between devices are 32-bit elements; how exact they have to be, the bound alone decides.
A program may use at most 64 MiB of HBM per device.

v0:
```python
import math

import jax
import jax.numpy as jnp
from jax import lax
from jax.sharding import PartitionSpec as P


def bit_parity(values):
    folded = jnp.bitwise_xor(values, jnp.right_shift(values, 16))
    folded = jnp.bitwise_xor(folded, jnp.right_shift(folded, 8))
    folded = jnp.bitwise_xor(folded, jnp.right_shift(folded, 4))
    folded = jnp.bitwise_xor(folded, jnp.right_shift(folded, 2))
    folded = jnp.bitwise_xor(folded, jnp.right_shift(folded, 1))
    return jnp.bitwise_and(folded, 1)


def hadamard(order_size):
    positions = lax.iota(jnp.int32, order_size)
    shared = jnp.bitwise_and(positions[:, None], positions[None, :])
    return jnp.where(bit_parity(shared) == 0, 1.0, -1.0).astype(jnp.float32)


def local(matrix_panel, row_signs, kept_rows):
    highest = lax.Precision.HIGHEST
    columns, local_rows = matrix_panel.shape
    outer_count = lax.axis_size("outer")
    inner_count = lax.axis_size("inner")
    device_count = outer_count * inner_count
    total_rows = local_rows * device_count
    me_outer = lax.axis_index("outer")
    me_inner = lax.axis_index("inner")
    signed = matrix_panel * row_signs.astype(jnp.float32)[None, :]
    leading = 128
    trailing = local_rows // leading
    blocks = signed.reshape(columns, leading, trailing)
    blocks = jnp.einsum("ap,jpq->jaq", hadamard(leading), blocks, precision=highest)
    blocks = jnp.einsum("bq,jaq->jab", hadamard(trailing), blocks, precision=highest)
    local_mix = blocks.reshape(columns, local_rows)
    low_bits = kept_rows % local_rows
    high_outer = kept_rows // (local_rows * inner_count)
    high_inner = kept_rows // local_rows % inner_count
    flips = bit_parity(jnp.bitwise_and(high_outer, me_outer)) + bit_parity(
        jnp.bitwise_and(high_inner, me_inner)
    )
    parity_sign = jnp.where(flips % 2 == 0, 1.0, -1.0).astype(jnp.float32)
    values = jnp.take(local_mix, low_bits, axis=1)
    summed = lax.psum_scatter(
        (values * parity_sign[None, :]).T, ("outer", "inner"), scatter_dimension=0, tiled=True
    )
    return summed * (1.0 / math.sqrt(total_rows))


def solution(mesh):
    return jax.shard_map(
        local,
        mesh=mesh,
        in_specs=(P(None, ("outer", "inner")), P(("outer", "inner")), P()),
        out_specs=P(("outer", "inner"), None),
        check_vma=False,
    )
```

profile of v0, /device:TPU:0, one launch (start us, length us, event | category | flops | bytes accessed | tf_op | source)
XLA Modules:
  0.0 171.1 jit_solution(15070143843797401162)
XLA Ops:
  6.5 0.0 reduce-scatter.2.cloned.1.call-start
  6.5 0.7 broadcast_clamp_fusion
  7.3 0.7 compare_and_fusion
  8.0 0.7 convert_element_type.3
  8.7 1.0 broadcast_multiply_fusion
  9.7 0.3 copy.8
  10.0 0.5 copy.9
  10.5 0.4 convolution_bitcast_fusion
  10.9 0.4 fusion.26
  11.3 0.5 copy.10
  11.9 10.8 %gather_fusion = f32[4096,32]{1,0:T(8,128)S(1)} fusion(f32[32,2048]{0,1:T(8,128)S(1)} %bitcast.12, s32[4096]{0:T(1024)S(1)} %broadcast_clamp_fusion), kind=kCustom, calls=%fused_computation | custom fusion | bytes 1064960 | tf_op jit(solution)/shard_map/jit(_take)/gather | solution.py:47
  22.6 0.0 copy-start
  22.6 0.6 copy.11
  23.2 0.1 copy-done
  23.4 0.1 fusion.22
  23.4 0.8 select_multiply_fusion
  24.2 0.0 reduce-scatter.2.cloned.1.call-update
  24.3 138.7 %reduce-scatter.2.cloned.1.call-done = f32[128,32]{0,1:T(8,128)} async-done(((f32[4096,32]{0,1:T(8,128)}), f32[128,32]{0,1:T(8,128)}) %reduce-scatter.2.cloned.1.call-update) | async-done | bytes 16400 | tf_op jit(solution)/shard_map/reduce_scatter | solution.py:48
  163.0 1.3 broadcast_multiply_fusion.1
Async XLA Ops:
  6.5 156.4 %reduce-scatter.2.cloned.1.call-start = ((), (), s32[]{:S(2)}) async-start(), calls=%async_computation.1 | async-start | bytes 540672 | tf_op jit(solution)/shard_map/reduce_scatter | solution.py:48
  22.6 0.7 copy-start
Sparse Core Ops, SparseCore 0:
  24.4 138.5 reduce-scatter.1
where the time goes:
time: 172 us; the launch traced here: 171 us
  waiting for transfers between devices  139 us (81%)
  between operations  13.5 us (8%)
  local copies, waits for them, and re-layouts  12.9 us (8%)
  other arithmetic  5.36 us (3%)
    reduce_scatter x1, waiting for transfers between devices, local(): lax.psum_scatter((values * parity_sign[None, :]).T, ('outer', 'inner'), s...  139 us
    gather x2, local copies, waits for them, and re-layouts, local(): values = jnp.take(local_mix, low_bits, axis=1)  11.3 us
  transfers between devices with their start and end apart: 1, of which 1 were waited for; matrix products, arithmetic and copies ran while one was open for 0% of the time, Pallas kernels for 0%

commit v1 on v0

--- a/solution.py
+++ b/solution.py
@@ -1,9 +1,16 @@
+import functools
 import math
 
 import jax
 import jax.numpy as jnp
 from jax import lax
+from jax.experimental import pallas as pl
+from jax.experimental.pallas import tpu as pltpu
 from jax.sharding import PartitionSpec as P
+
+MESH = pl.DeviceIdType.MESH
+LANES = 128
+SHARE = 4
 
 
 def bit_parity(values):
@@ -21,7 +28,7 @@
     return jnp.where(bit_parity(shared) == 0, 1.0, -1.0).astype(jnp.float32)
 
 
-def local(matrix_panel, row_signs, kept_rows):
+def scatter_form(matrix_panel, row_signs, kept_rows):
     highest = lax.Precision.HIGHEST
     columns, local_rows = matrix_panel.shape
     outer_count = lax.axis_size("outer")
@@ -51,7 +58,232 @@
     return summed * (1.0 / math.sqrt(total_rows))
 
 
+def flipped(index, mask, size):
+    result, bit = 0, 1
+    while bit < size:
+        digit = index // bit % 2
+        result = result + (1 - digit if mask & bit else digit) * bit
+        bit *= 2
+    return result
+
+
+def log2(size):
+    return size.bit_length() - 1
+
+
+def sign_of_bit(rows, bit):
+    return (1 - 2 * jnp.bitwise_and(jnp.right_shift(rows, bit), 1)).astype(jnp.float32)
+
+
+def kernel(
+    outer_count, inner_count, low_count, scale,
+    panel_ref, signs_ref, kept_ref, out_ref,
+    send1, recv1, send2, recv2, mix_ref, bits_ref, final_ref,
+    send1_sem, recv1_sem, send2_sem, recv2_sem,
+):
+    device_count = outer_count * inner_count
+    high_count = inner_count // low_count
+    group = outer_count * low_count
+    columns, local_rows = panel_ref.shape
+    kept_count = kept_ref.shape[1]
+    mids = local_rows // LANES
+    rows = mids * SHARE
+    me_outer = lax.axis_index("outer")
+    me_inner = lax.axis_index("inner")
+    me = me_outer * inner_count + me_inner
+    me_high = me_inner // low_count
+    me_low = me_inner % low_count
+    me_group = me_outer * low_count + me_low
+
+    barrier = pltpu.get_barrier_semaphore()
+
+    def greet(step, carry):
+        other = (me + step) % device_count
+        pl.semaphore_signal(
+            barrier, inc=1, device_id=(other // inner_count, other % inner_count), device_id_type=MESH
+        )
+        return carry
+
+    lax.fori_loop(1, device_count, greet, 0)
+
+    for mid in range(mids):
+        lanes = slice(mid * LANES, (mid + 1) * LANES)
+        block = panel_ref[:, lanes] * signs_ref[:, lanes].astype(jnp.float32)
+        for peer in range(group):
+            send1[peer, mid * SHARE:(mid + 1) * SHARE, :] = block[peer * SHARE:(peer + 1) * SHARE, :]
+
+    pl.semaphore_wait(barrier, device_count - 1)
+
+    copies = []
+    for mask in sorted(range(1, group), key=lambda m: (-bin(m).count("1"), -m)):
+        peer = flipped(me_group, mask, group)
+        copy = pltpu.make_async_remote_copy(
+            src_ref=send1.at[peer],
+            dst_ref=recv1.at[me_group],
+            send_sem=send1_sem.at[mask],
+            recv_sem=recv1_sem.at[mask],
+            device_id=(peer // low_count, me_high * low_count + peer % low_count),
+            device_id_type=MESH,
+        )
+        copy.start()
+        copies.append(copy)
+    recv1[me_group] = send1[me_group]
+
+    span = 4 * LANES
+    low_bits = log2(LANES)
+    inner_bits = log2(inner_count)
+    fold_bits = [log2(local_rows) + inner_bits + b for b in reversed(range(log2(outer_count)))]
+    fold_bits += [log2(local_rows) + b for b in reversed(range(log2(low_count)))]
+    fold_bits += [b for b in reversed(range(low_bits, log2(local_rows)))]
+
+    def signs_of(chunk, carry):
+        lanes = pl.ds(pl.multiple_of(chunk * span, span), span)
+        kept = kept_ref[:, lanes]
+        for place, bit in enumerate(fold_bits):
+            bits_ref[place:place + 1, lanes] = sign_of_bit(kept, bit)
+        position = lax.broadcasted_iota(jnp.int32, (16, span), 0)
+        base = jnp.ones((16, span), jnp.float32)
+        for bit in range(4):
+            taken = jnp.bitwise_and(jnp.right_shift(position, bit), 1) == 1
+            base = base * jnp.where(taken, sign_of_bit(kept, bit), 1.0)
+        for top in range(LANES // 16):
+            block = base
+            for bit in range(4, low_bits):
+                if top >> (bit - 4) & 1:
+                    block = block * sign_of_bit(kept, bit)
+            block = block.astype(jnp.bfloat16)
+            mix_ref[top * 16:(top + 1) * 16, lanes] = block
+            mix_ref[LANES + top * 16:LANES + (top + 1) * 16, lanes] = block
+        return carry
+
+    lax.fori_loop(0, kept_count // span, signs_of, 0)
+
+    for copy in copies:
+        copy.wait_recv()
+
+    gathered = recv1[...].reshape(group * rows, LANES)
+    upper = gathered.astype(jnp.bfloat16)
+    lower = (gathered - upper.astype(jnp.float32)).astype(jnp.bfloat16)
+    both = jnp.concatenate([upper, lower], axis=1)
+
+    mine = me_high * group + me_group
+    width = low_count * LANES
+    far = [(h, o) for h in reversed(range(high_count)) for o in reversed(range(outer_count))]
+    sent = []
+    for high_mask, outer_mask in far:
+        high = flipped(me_high, high_mask, high_count)
+        outer = flipped(me_outer, outer_mask, outer_count)
+        block = outer * high_count + high
+        lanes = pl.ds(pl.multiple_of(block * width, width), width)
+        part = jnp.dot(both, mix_ref[:, lanes], preferred_element_type=jnp.float32)
+        for place in range(len(fold_bits)):
+            half = part.shape[0] // 2
+            part = part[:half] + part[half:] * bits_ref[place:place + 1, lanes]
+        for low in range(low_count):
+            to = block * low_count + low
+            piece = part[:, low * LANES:(low + 1) * LANES]
+            send2[to] = piece
+            copy = pltpu.make_async_remote_copy(
+                src_ref=send2.at[to],
+                dst_ref=recv2.at[mine],
+                send_sem=send2_sem.at[to],
+                recv_sem=recv2_sem.at[mine],
+                device_id=(outer, high * low_count + low),
+                device_id_type=MESH,
+            )
+            if high_mask == 0 and outer_mask == 0:
+                @pl.when(low == me_low)
+                def _():
+                    recv2[mine] = piece
+
+                @pl.when(low != me_low)
+                def _():
+                    copy.start()
+            else:
+                copy.start()
+
+    kept = kept_ref[:, pl.ds(pl.multiple_of(me * LANES, LANES), LANES)]
+    high_signs = [sign_of_bit(kept, log2(local_rows * low_count) + b) for b in range(log2(high_count))]
+
+    def arrival(source):
+        return pltpu.make_async_remote_copy(
+            src_ref=send2.at[source],
+            dst_ref=recv2.at[source],
+            send_sem=send2_sem.at[source],
+            recv_sem=recv2_sem.at[source],
+            device_id=(me_outer, me_inner),
+            device_id_type=MESH,
+        )
+
+    def await_arrival(step, carry):
+        arrival((mine + step) % device_count).wait_recv()
+        return carry
+
+    lax.fori_loop(1, device_count, await_arrival, 0)
+
+    for peer in range(group):
+        total = recv2[peer]
+        for high in range(1, high_count):
+            term = recv2[high * group + peer]
+            for bit, sign in enumerate(high_signs):
+                if high >> bit & 1:
+                    term = term * sign
+            total = total + term
+        final_ref[peer * SHARE:(peer + 1) * SHARE, :] = total * scale
+    out_ref[...] = final_ref[...].T
+
+    def await_sent(step, carry):
+        arrival((me + step) % device_count).wait_send()
+        return carry
+
+    lax.fori_loop(1, device_count, await_sent, 0)
+    for copy in copies:
+        copy.wait_send()
+
+
 def solution(mesh):
+    outer_count, inner_count = mesh.shape["outer"], mesh.shape["inner"]
+    device_count = outer_count * inner_count
+
+    def local(matrix_panel, row_signs, kept_rows):
+        columns, local_rows = matrix_panel.shape
+        kept_count = kept_rows.shape[0]
+        low_count = max(columns // (SHARE * outer_count), 1)
+        fits = (
+            low_count * outer_count * SHARE == columns
+            and inner_count % low_count == 0
+            and kept_count == device_count * LANES
+            and local_rows % (2 * LANES) == 0
+        )
+        if not fits:
+            return scatter_form(matrix_panel, row_signs, kept_rows)
+        group = outer_count * low_count
+        rows = local_rows // LANES * SHARE
+        bits = log2(group) + log2(local_rows // LANES)
+        in_vmem = pl.BlockSpec(memory_space=pltpu.VMEM)
+        return pl.pallas_call(
+            functools.partial(
+                kernel, outer_count, inner_count, low_count, 1.0 / math.sqrt(local_rows * device_count)
+            ),
+            out_shape=jax.ShapeDtypeStruct((LANES, columns), jnp.float32),
+            in_specs=[in_vmem] * 3,
+            out_specs=in_vmem,
+            scratch_shapes=[
+                pltpu.VMEM((group, rows, LANES), jnp.float32),
+                pltpu.VMEM((group, rows, LANES), jnp.float32),
+                pltpu.VMEM((device_count, SHARE, LANES), jnp.float32),
+                pltpu.VMEM((device_count, SHARE, LANES), jnp.float32),
+                pltpu.VMEM((2 * LANES, kept_count), jnp.bfloat16),
+                pltpu.VMEM((bits, kept_count), jnp.float32),
+                pltpu.VMEM((columns, LANES), jnp.float32),
+                pltpu.SemaphoreType.DMA((group,)),
+                pltpu.SemaphoreType.DMA((group,)),
+                pltpu.SemaphoreType.DMA((device_count,)),
+                pltpu.SemaphoreType.DMA((device_count,)),
+            ],
+            compiler_params=pltpu.CompilerParams(collective_id=0, has_side_effects=True),
+        )(matrix_panel, row_signs.reshape(1, local_rows), kept_rows.reshape(1, kept_count))
+
     return jax.shard_map(
         local,
         mesh=mesh,

time: 172 us -> 24.1 us (0.14)
  waiting for transfers between devices: 139 us -> 0 us
  Pallas kernels: 0 us -> 22.4 us
  between operations: 13.5 us -> 0.01 us
  local copies, waits for them, and re-layouts: 12.9 us -> 1.52 us
  other arithmetic: 5.36 us -> 0 us
    reduce_scatter x1 -> x0, waiting for transfers between devices: 139 us -> none  [local(): lax.psum_scatter((values * parity_sign[None, :]).T, ('outer', 'inner'), s...]
    pallas_call x0 -> x1, Pallas kernels: none -> 22.4 us  [local(): pl.pallas_call(functools.partial(kernel, outer_count, inner_count, low_co...]
    gather x2 -> x0, local copies, waits for them, and re-layouts: 11.3 us -> none  [local(): values = jnp.take(local_mix, low_bits, axis=1)]
    mul x3 -> x0, other arithmetic: 3.13 us -> none  [the longest x1 1.32 us: local(): return summed * (1.0 / math.sqrt(total_rows))]
  transfers between devices with their start and end apart: 1 -> 0, of which waited for: 1 -> 0; matrix products, arithmetic and copies ran while one was open for 0% -> 0% of each run, Pallas kernels for 0% -> 0%
where the time goes in v1:
time: 24.1 us; the launch traced here: 23.9 us
  Pallas kernels  22.4 us (93%)
  local copies, waits for them, and re-layouts  1.52 us (6%)
    pallas_call x1, Pallas kernels, local(): pl.pallas_call(functools.partial(kernel, outer_count, inner_count, low_co...  22.4 us
    pallas_call x1, local copies, waits for them, and re-layouts, local(): pl.pallas_call(functools.partial(kernel, outer_count, inner_count, low_co...  1.52 us

profile of v1, /device:TPU:0, one launch (start us, length us, event | category | flops | bytes accessed | tf_op | source)
XLA Modules:
  0.0 23.9 jit_solution(6771959791283649167)
XLA Ops:
  0.0 22.4 %shard_map.37 = f32[128,32]{1,0:T(8,128)} custom-call(f32[32,2048]{1,0:T(8,128)} %panel_ref.1, s32[1,2048]{1,0:T(1,128)} %bitcast.3, s32[1,4096]{1,0:T(1,128)} %bitcast.2), custom_call_target="tpu_custom_call" | custom-call | tf_op jit(solution)/shard_map/pallas_call | solution.py:264
  22.4 1.5 %copy.4 = f32[128,32]{0,1:T(8,128)} copy(f32[128,32]{1,0:T(8,128)} %shard_map.37) | data formatting | bytes 32768 | tf_op jit(solution)/shard_map/pallas_call | solution.py:264

commit v2 on v1

--- a/solution.py
+++ b/solution.py
@@ -77,15 +77,16 @@
 
 def kernel(
     outer_count, inner_count, low_count, scale,
-    panel_ref, signs_ref, kept_ref, out_ref,
+    panel_hbm, signs_hbm, kept_hbm, out_ref,
+    panel_ref, signs_ref, kept_ref, load_sem, ready_sem,
     send1, recv1, send2, recv2, mix_ref, bits_ref, final_ref,
     send1_sem, recv1_sem, send2_sem, recv2_sem,
 ):
     device_count = outer_count * inner_count
     high_count = inner_count // low_count
     group = outer_count * low_count
-    columns, local_rows = panel_ref.shape
-    kept_count = kept_ref.shape[1]
+    columns, local_rows = panel_hbm.shape
+    kept_count = kept_hbm.shape[1]
     mids = local_rows // LANES
     rows = mids * SHARE
     me_outer = lax.axis_index("outer")
@@ -97,14 +98,33 @@
 
     barrier = pltpu.get_barrier_semaphore()
 
-    def greet(step, carry):
-        other = (me + step) % device_count
+    loads = [
+        pltpu.make_async_copy(source, target, load_sem.at[place])
+        for place, (source, target) in enumerate(
+            [(panel_hbm, panel_ref), (signs_hbm, signs_ref), (kept_hbm, kept_ref)]
+        )
+    ]
+    for load in loads:
+        load.start()
+
+    def tell_group(semaphore):
+        for step in range(1, group):
+            peer = (me_group + step) % group
+            pl.semaphore_signal(
+                semaphore,
+                inc=1,
+                device_id=(peer // low_count, me_high * low_count + peer % low_count),
+                device_id_type=MESH,
+            )
+
+    for step in range(1, high_count):
+        high = (me_high + step) % high_count
         pl.semaphore_signal(
-            barrier, inc=1, device_id=(other // inner_count, other % inner_count), device_id_type=MESH
-        )
-        return carry
-
-    lax.fori_loop(1, device_count, greet, 0)
+            barrier, inc=1, device_id=(me_outer, high * low_count + me_low), device_id_type=MESH
+        )
+    tell_group(barrier)
+    for load in loads:
+        load.wait()
 
     for mid in range(mids):
         lanes = slice(mid * LANES, (mid + 1) * LANES)
@@ -112,7 +132,7 @@
         for peer in range(group):
             send1[peer, mid * SHARE:(mid + 1) * SHARE, :] = block[peer * SHARE:(peer + 1) * SHARE, :]
 
-    pl.semaphore_wait(barrier, device_count - 1)
+    pl.semaphore_wait(barrier, group - 1 + high_count - 1)
 
     copies = []
     for mask in sorted(range(1, group), key=lambda m: (-bin(m).count("1"), -m)):
@@ -127,6 +147,7 @@
         )
         copy.start()
         copies.append(copy)
+    tell_group(ready_sem)
     recv1[me_group] = send1[me_group]
 
     span = 4 * LANES
@@ -166,6 +187,7 @@
     lower = (gathered - upper.astype(jnp.float32)).astype(jnp.bfloat16)
     both = jnp.concatenate([upper, lower], axis=1)
 
+    pl.semaphore_wait(ready_sem, group - 1)
     mine = me_high * group + me_group
     width = low_count * LANES
     far = [(h, o) for h in reversed(range(high_count)) for o in reversed(range(outer_count))]
@@ -230,7 +252,7 @@
                     term = term * sign
             total = total + term
         final_ref[peer * SHARE:(peer + 1) * SHARE, :] = total * scale
-    out_ref[...] = final_ref[...].T
+    out_ref[...] = final_ref[...]
 
     def await_sent(step, carry):
         arrival((me + step) % device_count).wait_send()
@@ -265,10 +287,15 @@
             functools.partial(
                 kernel, outer_count, inner_count, low_count, 1.0 / math.sqrt(local_rows * device_count)
             ),
-            out_shape=jax.ShapeDtypeStruct((LANES, columns), jnp.float32),
-            in_specs=[in_vmem] * 3,
+            out_shape=jax.ShapeDtypeStruct((columns, LANES), jnp.float32),
+            in_specs=[pl.BlockSpec(memory_space=pl.ANY)] * 3,
             out_specs=in_vmem,
             scratch_shapes=[
+                pltpu.VMEM((columns, local_rows), jnp.float32),
+                pltpu.VMEM((1, local_rows), jnp.int32),
+                pltpu.VMEM((1, kept_count), jnp.int32),
+                pltpu.SemaphoreType.DMA((3,)),
+                pltpu.SemaphoreType.REGULAR,
                 pltpu.VMEM((group, rows, LANES), jnp.float32),
                 pltpu.VMEM((group, rows, LANES), jnp.float32),
                 pltpu.VMEM((device_count, SHARE, LANES), jnp.float32),
@@ -282,7 +309,7 @@
                 pltpu.SemaphoreType.DMA((device_count,)),
             ],
             compiler_params=pltpu.CompilerParams(collective_id=0, has_side_effects=True),
-        )(matrix_panel, row_signs.reshape(1, local_rows), kept_rows.reshape(1, kept_count))
+        )(matrix_panel, row_signs.reshape(1, local_rows), kept_rows.reshape(1, kept_count)).T
 
     return jax.shard_map(
         local,

time: 24.1 us -> 21.5 us (0.89)
  Pallas kernels: 22.4 us -> 19.9 us
    pallas_call x1, Pallas kernels: 22.4 us -> 19.9 us  [local(): pl.pallas_call(functools.partial(kernel, outer_count, inner_count, low_co...]
    pallas_call x1 -> x0, local copies, waits for them, and re-layouts: 1.52 us -> none  [local(): pl.pallas_call(functools.partial(kernel, outer_count, inner_count, low_co...]
    unnamed x0 -> x1, local copies, waits for them, and re-layouts: none -> 1.32 us
where the time goes in v2:
time: 21.5 us; the launch traced here: 21.2 us
  Pallas kernels  19.9 us (93%)
  local copies, waits for them, and re-layouts  1.32 us (6%)
    pallas_call x1, Pallas kernels, local(): pl.pallas_call(functools.partial(kernel, outer_count, inner_count, low_co...  19.9 us
    unnamed x1, local copies, waits for them, and re-layouts  1.32 us

profile of v2, /device:TPU:0, one launch (start us, length us, event | category | flops | bytes accessed | tf_op | source)
XLA Modules:
  0.0 21.2 jit_solution(79377683450508340)
XLA Ops:
  0.0 19.9 %shard_map.37 = f32[32,128]{1,0:T(8,128)} custom-call(f32[32,2048]{1,0:T(8,128)} %panel_hbm.1, s32[1,2048]{1,0:T(1,128)} %bitcast.5, s32[1,4096]{1,0:T(1,128)} %bitcast.4), custom_call_target="tpu_custom_call" | custom-call | tf_op jit(solution)/shard_map/pallas_call | solution.py:286
  19.9 1.3 %copy.5 = f32[128,32]{0,1:T(8,128)} copy(f32[128,32]{0,1:T(8,128)} %bitcast.3) | data formatting | bytes 32768

commit v3 on v2

--- a/solution.py
+++ b/solution.py
@@ -77,10 +77,10 @@
 
 def kernel(
     outer_count, inner_count, low_count, scale,
-    panel_hbm, signs_hbm, kept_hbm, out_ref,
+    panel_hbm, signs_hbm, kept_hbm, recv2,
     panel_ref, signs_ref, kept_ref, load_sem, ready_sem,
-    send1, recv1, send2, recv2, mix_ref, bits_ref, final_ref,
-    send1_sem, recv1_sem, send2_sem, recv2_sem,
+    send1, recv1, send2, mix_ref, bits_ref,
+    send1_sem, recv1_sem, send2_sem, recv2_sem, own_sem,
 ):
     device_count = outer_count * inner_count
     high_count = inner_count // low_count
@@ -135,7 +135,7 @@
     pl.semaphore_wait(barrier, group - 1 + high_count - 1)
 
     copies = []
-    for mask in sorted(range(1, group), key=lambda m: (-bin(m).count("1"), -m)):
+    for mask in sorted(range(1, group), key=lambda m: (bin(m).count("1"), m)):
         peer = flipped(me_group, mask, group)
         copy = pltpu.make_async_remote_copy(
             src_ref=send1.at[peer],
@@ -162,6 +162,12 @@
         kept = kept_ref[:, lanes]
         for place, bit in enumerate(fold_bits):
             bits_ref[place:place + 1, lanes] = sign_of_bit(kept, bit)
+        plane = jnp.full((1, span), scale, jnp.float32)
+        for bit in range(log2(high_count)):
+            here = me_high // (1 << bit) % 2
+            flip = sign_of_bit(kept, log2(local_rows * low_count) + bit)
+            plane = plane * jnp.where(here == 1, flip, 1.0)
+        bits_ref[len(fold_bits):len(fold_bits) + 1, lanes] = plane
         position = lax.broadcasted_iota(jnp.int32, (16, span), 0)
         base = jnp.ones((16, span), jnp.float32)
         for bit in range(4):
@@ -201,10 +207,10 @@
         for place in range(len(fold_bits)):
             half = part.shape[0] // 2
             part = part[:half] + part[half:] * bits_ref[place:place + 1, lanes]
+        part = part * bits_ref[len(fold_bits):len(fold_bits) + 1, lanes]
         for low in range(low_count):
             to = block * low_count + low
-            piece = part[:, low * LANES:(low + 1) * LANES]
-            send2[to] = piece
+            send2[to] = part[:, low * LANES:(low + 1) * LANES]
             copy = pltpu.make_async_remote_copy(
                 src_ref=send2.at[to],
                 dst_ref=recv2.at[mine],
@@ -214,18 +220,13 @@
                 device_id_type=MESH,
             )
             if high_mask == 0 and outer_mask == 0:
-                @pl.when(low == me_low)
-                def _():
-                    recv2[mine] = piece
-
                 @pl.when(low != me_low)
                 def _():
                     copy.start()
             else:
                 copy.start()
-
-    kept = kept_ref[:, pl.ds(pl.multiple_of(me * LANES, LANES), LANES)]
-    high_signs = [sign_of_bit(kept, log2(local_rows * low_count) + b) for b in range(log2(high_count))]
+    own = pltpu.make_async_copy(send2.at[me], recv2.at[mine], own_sem)
+    own.start()
 
     def arrival(source):
         return pltpu.make_async_remote_copy(
@@ -243,17 +244,6 @@
 
     lax.fori_loop(1, device_count, await_arrival, 0)
 
-    for peer in range(group):
-        total = recv2[peer]
-        for high in range(1, high_count):
-            term = recv2[high * group + peer]
-            for bit, sign in enumerate(high_signs):
-                if high >> bit & 1:
-                    term = term * sign
-            total = total + term
-        final_ref[peer * SHARE:(peer + 1) * SHARE, :] = total * scale
-    out_ref[...] = final_ref[...]
-
     def await_sent(step, carry):
         arrival((me + step) % device_count).wait_send()
         return carry
@@ -261,6 +251,7 @@
     lax.fori_loop(1, device_count, await_sent, 0)
     for copy in copies:
         copy.wait_send()
+    own.wait()
 
 
 def solution(mesh):
@@ -282,14 +273,13 @@
         group = outer_count * low_count
         rows = local_rows // LANES * SHARE
         bits = log2(group) + log2(local_rows // LANES)
-        in_vmem = pl.BlockSpec(memory_space=pltpu.VMEM)
-        return pl.pallas_call(
+        arrived = pl.pallas_call(
             functools.partial(
                 kernel, outer_count, inner_count, low_count, 1.0 / math.sqrt(local_rows * device_count)
             ),
-            out_shape=jax.ShapeDtypeStruct((columns, LANES), jnp.float32),
+            out_shape=jax.ShapeDtypeStruct((device_count, SHARE, LANES), jnp.float32),
             in_specs=[pl.BlockSpec(memory_space=pl.ANY)] * 3,
-            out_specs=in_vmem,
+            out_specs=pl.BlockSpec(memory_space=pl.ANY),
             scratch_shapes=[
                 pltpu.VMEM((columns, local_rows), jnp.float32),
                 pltpu.VMEM((1, local_rows), jnp.int32),
@@ -299,17 +289,18 @@
                 pltpu.VMEM((group, rows, LANES), jnp.float32),
                 pltpu.VMEM((group, rows, LANES), jnp.float32),
                 pltpu.VMEM((device_count, SHARE, LANES), jnp.float32),
-                pltpu.VMEM((device_count, SHARE, LANES), jnp.float32),
                 pltpu.VMEM((2 * LANES, kept_count), jnp.bfloat16),
-                pltpu.VMEM((bits, kept_count), jnp.float32),
-                pltpu.VMEM((columns, LANES), jnp.float32),
+                pltpu.VMEM((bits + 1, kept_count), jnp.float32),
                 pltpu.SemaphoreType.DMA((group,)),
                 pltpu.SemaphoreType.DMA((group,)),
                 pltpu.SemaphoreType.DMA((device_count,)),
                 pltpu.SemaphoreType.DMA((device_count,)),
+                pltpu.SemaphoreType.DMA(()),
             ],
             compiler_params=pltpu.CompilerParams(collective_id=0, has_side_effects=True),
-        )(matrix_panel, row_signs.reshape(1, local_rows), kept_rows.reshape(1, kept_count)).T
+        )(matrix_panel, row_signs.reshape(1, local_rows), kept_rows.reshape(1, kept_count))
+        planes = arrived.reshape(device_count // group, columns, LANES)
+        return jnp.sum(planes, axis=0).T
 
     return jax.shard_map(
         local,

time: 21.5 us -> 20.7 us (0.963)
  other arithmetic: 0 us -> 1.45 us
  local copies, waits for them, and re-layouts: 1.32 us -> 0 us
  Pallas kernels: 19.9 us -> 19.1 us
    reduce_sum x0 -> x1, other arithmetic: none -> 1.45 us  [local(): return jnp.sum(planes, axis=0).T]
    unnamed x1 -> x0, local copies, waits for them, and re-layouts: 1.32 us -> none
    pallas_call x1, Pallas kernels: 19.9 us -> 19.1 us  [local(): pl.pallas_call(functools.partial(kernel, outer_count, inner_count, low_co...]
where the time goes in v3:
time: 20.7 us; the launch traced here: 20.6 us
  Pallas kernels  19.1 us (92%)
  other arithmetic  1.45 us (7%)
    pallas_call x1, Pallas kernels, local(): pl.pallas_call(functools.partial(kernel, outer_count, inner_count, low_co...  19.1 us
    reduce_sum x1, other arithmetic, local(): return jnp.sum(planes, axis=0).T  1.45 us

profile of v3, /device:TPU:0, one launch (start us, length us, event | category | flops | bytes accessed | tf_op | source)
XLA Modules:
  0.0 20.6 jit_solution(11245910703765204650)
XLA Ops:
  0.0 19.1 %shard_map.37 = f32[32,4,128]{2,1,0:T(4,128)} custom-call(f32[32,2048]{1,0:T(8,128)} %panel_hbm.1, s32[1,2048]{1,0:T(1,128)} %bitcast.8, s32[1,4096]{1,0:T(1,128)} %bitcast.7), custom_call_target="tpu_custom_call" | custom-call | tf_op jit(solution)/shard_map/pallas_call | solution.py:276
  19.1 1.5 %bitcast_reduce_fusion = f32[32,128]{1,0:T(8,128)} fusion(f32[4,32,128]{2,1,0:T(8,128)} %bitcast.6), kind=kLoop, calls=%fused_computation | loop fusion | flops 12288 | bytes 81920 | tf_op jit(solution)/shard_map/reduce_sum | solution.py:303

commit v4 on v3

--- a/solution.py
+++ b/solution.py
@@ -197,34 +197,50 @@
     mine = me_high * group + me_group
     width = low_count * LANES
     far = [(h, o) for h in reversed(range(high_count)) for o in reversed(range(outer_count))]
-    sent = []
-    for high_mask, outer_mask in far:
-        high = flipped(me_high, high_mask, high_count)
-        outer = flipped(me_outer, outer_mask, outer_count)
-        block = outer * high_count + high
-        lanes = pl.ds(pl.multiple_of(block * width, width), width)
-        part = jnp.dot(both, mix_ref[:, lanes], preferred_element_type=jnp.float32)
-        for place in range(len(fold_bits)):
-            half = part.shape[0] // 2
-            part = part[:half] + part[half:] * bits_ref[place:place + 1, lanes]
-        part = part * bits_ref[len(fold_bits):len(fold_bits) + 1, lanes]
-        for low in range(low_count):
-            to = block * low_count + low
-            send2[to] = part[:, low * LANES:(low + 1) * LANES]
-            copy = pltpu.make_async_remote_copy(
-                src_ref=send2.at[to],
-                dst_ref=recv2.at[mine],
-                send_sem=send2_sem.at[to],
-                recv_sem=recv2_sem.at[mine],
-                device_id=(outer, high * low_count + low),
-                device_id_type=MESH,
-            )
-            if high_mask == 0 and outer_mask == 0:
-                @pl.when(low != me_low)
-                def _():
+    together = 2
+    for first in range(0, len(far), together):
+        places = []
+        for high_mask, outer_mask in far[first:first + together]:
+            high = flipped(me_high, high_mask, high_count)
+            outer = flipped(me_outer, outer_mask, outer_count)
+            block = outer * high_count + high
+            lanes = pl.ds(pl.multiple_of(block * width, width), width)
+            places.append((high_mask == 0 and outer_mask == 0, high, outer, block, lanes))
+        parts = [
+            jnp.dot(both, mix_ref[:, place[4]], preferred_element_type=jnp.float32) for place in places
+        ]
+        signs = [
+            [jnp.broadcast_to(bits_ref[bit:bit + 1, place[4]], (2 * SHARE, width)) for bit in range(len(fold_bits) + 1)]
+            for place in places
+        ]
+
+        def fold(start, size, bit):
+            if size == 2 * SHARE:
+                return [part[start:start + size] for part in parts]
+            half = size // 2
+            left, right = fold(start, half, bit + 1), fold(start + half, half, bit + 1)
+            return [a + b * sign[bit] for a, b, sign in zip(left, right, signs)]
+
+        for (last, high, outer, block, lanes), tile, sign in zip(places, fold(0, group * rows, 0), signs):
+            bit = len(fold_bits) - 1
+            part = (tile[:SHARE] + tile[SHARE:] * sign[bit][:SHARE]) * sign[bit + 1][:SHARE]
+            for low in range(low_count):
+                to = block * low_count + low
+                send2[to] = part[:, low * LANES:(low + 1) * LANES]
+                copy = pltpu.make_async_remote_copy(
+                    src_ref=send2.at[to],
+                    dst_ref=recv2.at[mine],
+                    send_sem=send2_sem.at[to],
+                    recv_sem=recv2_sem.at[mine],
+                    device_id=(outer, high * low_count + low),
+                    device_id_type=MESH,
+                )
+                if last:
+                    @pl.when(low != me_low)
+                    def _(copy=copy):
+                        copy.start()
+                else:
                     copy.start()
-            else:
-                copy.start()
     own = pltpu.make_async_copy(send2.at[me], recv2.at[mine], own_sem)
     own.start()
 

time: 20.7 us -> 18.5 us (0.89)
  Pallas kernels: 19.1 us -> 16.9 us
    pallas_call x1, Pallas kernels: 19.1 us -> 16.9 us  [local(): pl.pallas_call(functools.partial(kernel, outer_count, inner_count, low_co...]
where the time goes in v4:
time: 18.5 us; the launch traced here: 18.4 us
  Pallas kernels  16.9 us (91%)
  other arithmetic  1.45 us (8%)
    pallas_call x1, Pallas kernels, local(): pl.pallas_call(functools.partial(kernel, outer_count, inner_count, low_co...  16.9 us
    reduce_sum x1, other arithmetic, local(): return jnp.sum(planes, axis=0).T  1.45 us

profile of v4, /device:TPU:0, one launch (start us, length us, event | category | flops | bytes accessed | tf_op | source)
XLA Modules:
  0.0 18.4 jit_solution(1130600863009639258)
XLA Ops:
  0.0 16.9 %shard_map.37 = f32[32,4,128]{2,1,0:T(4,128)} custom-call(f32[32,2048]{1,0:T(8,128)} %panel_hbm.1, s32[1,2048]{1,0:T(1,128)} %bitcast.8, s32[1,4096]{1,0:T(1,128)} %bitcast.7), custom_call_target="tpu_custom_call" | custom-call | tf_op jit(solution)/shard_map/pallas_call | solution.py:292
  16.9 1.5 %bitcast_reduce_fusion = f32[32,128]{1,0:T(8,128)} fusion(f32[4,32,128]{2,1,0:T(8,128)} %bitcast.6), kind=kLoop, calls=%fused_computation | loop fusion | flops 12288 | bytes 81920 | tf_op jit(solution)/shard_map/reduce_sum | solution.py:319

commit v5 on v4

--- a/solution.py
+++ b/solution.py
@@ -78,7 +78,7 @@
 def kernel(
     outer_count, inner_count, low_count, scale,
     panel_hbm, signs_hbm, kept_hbm, recv2,
-    panel_ref, signs_ref, kept_ref, load_sem, ready_sem,
+    panel_ref, signs_ref, kept_ref, load_sem, ready_sem, line_sem,
     send1, recv1, send2, mix_ref, bits_ref,
     send1_sem, recv1_sem, send2_sem, recv2_sem, own_sem,
 ):
@@ -117,11 +117,18 @@
                 device_id_type=MESH,
             )
 
-    for step in range(1, high_count):
-        high = (me_high + step) % high_count
-        pl.semaphore_signal(
-            barrier, inc=1, device_id=(me_outer, high * low_count + me_low), device_id_type=MESH
-        )
+    def tell_line(semaphore):
+        for step in (-1, 1):
+            high = me_high + step
+
+            @pl.when((high >= 0) & (high < high_count))
+            def _(high=high):
+                pl.semaphore_signal(
+                    semaphore, inc=1, device_id=(me_outer, high * low_count + me_low), device_id_type=MESH
+                )
+
+    line = jnp.where(me_high > 0, 1, 0) + jnp.where(me_high < high_count - 1, 1, 0)
+    tell_line(barrier)
     tell_group(barrier)
     for load in loads:
         load.wait()
@@ -132,7 +139,7 @@
         for peer in range(group):
             send1[peer, mid * SHARE:(mid + 1) * SHARE, :] = block[peer * SHARE:(peer + 1) * SHARE, :]
 
-    pl.semaphore_wait(barrier, group - 1 + high_count - 1)
+    pl.semaphore_wait(barrier, group - 1 + line)
 
     copies = []
     for mask in sorted(range(1, group), key=lambda m: (bin(m).count("1"), m)):
@@ -147,7 +154,6 @@
         )
         copy.start()
         copies.append(copy)
-    tell_group(ready_sem)
     recv1[me_group] = send1[me_group]
 
     span = 4 * LANES
@@ -183,7 +189,15 @@
             mix_ref[LANES + top * 16:LANES + (top + 1) * 16, lanes] = block
         return carry
 
-    lax.fori_loop(0, kept_count // span, signs_of, 0)
+    rounds = max(high_count - 2, 0)
+    spans = kept_count // span
+    for turn in range(rounds):
+        tell_line(line_sem.at[turn])
+        lax.fori_loop(spans * turn // rounds, spans * (turn + 1) // rounds, signs_of, 0)
+        pl.semaphore_wait(line_sem.at[turn], line)
+    if not rounds:
+        lax.fori_loop(0, spans, signs_of, 0)
+    tell_group(ready_sem)
 
     for copy in copies:
         copy.wait_recv()
@@ -302,6 +316,7 @@
                 pltpu.VMEM((1, kept_count), jnp.int32),
                 pltpu.SemaphoreType.DMA((3,)),
                 pltpu.SemaphoreType.REGULAR,
+                pltpu.SemaphoreType.REGULAR((max(inner_count // low_count - 2, 1),)),
                 pltpu.VMEM((group, rows, LANES), jnp.float32),
                 pltpu.VMEM((group, rows, LANES), jnp.float32),
                 pltpu.VMEM((device_count, SHARE, LANES), jnp.float32),

time: 18.5 us -> 18.2 us (0.984)
  Pallas kernels: 16.9 us -> 16.5 us
    pallas_call x1, Pallas kernels: 16.9 us -> 16.5 us  [local(): pl.pallas_call(functools.partial(kernel, outer_count, inner_count, low_co...]
where the time goes in v5:
time: 18.2 us; the launch traced here: 18 us
  Pallas kernels  16.5 us (91%)
  other arithmetic  1.45 us (8%)
    pallas_call x1, Pallas kernels, local(): pl.pallas_call(functools.partial(kernel, outer_count, inner_count, low_co...  16.5 us
    reduce_sum x1, other arithmetic, local(): return jnp.sum(planes, axis=0).T  1.45 us

profile of v5, /device:TPU:0, one launch (start us, length us, event | category | flops | bytes accessed | tf_op | source)
XLA Modules:
  0.0 18.0 jit_solution(5222336613403329427)
XLA Ops:
  0.0 16.5 %shard_map.37 = f32[32,4,128]{2,1,0:T(4,128)} custom-call(f32[32,2048]{1,0:T(8,128)} %panel_hbm.1, s32[1,2048]{1,0:T(1,128)} %bitcast.8, s32[1,4096]{1,0:T(1,128)} %bitcast.7), custom_call_target="tpu_custom_call" | custom-call | tf_op jit(solution)/shard_map/pallas_call | solution.py:306
  16.5 1.5 %bitcast_reduce_fusion = f32[32,128]{1,0:T(8,128)} fusion(f32[4,32,128]{2,1,0:T(8,128)} %bitcast.6), kind=kLoop, calls=%fused_computation | loop fusion | flops 12288 | bytes 81920 | tf_op jit(solution)/shard_map/reduce_sum | solution.py:334
